TPU v7x, 32 devices: a whole 2x2x4 slice. The times are simulated.
32 devices in a mesh: layer: 2 (over y), row: 4 (over z), col: 4 (over x, core).
Axes of the slice: x: 2, y: 2, z: 4, core: 2. Of those that a mesh axis runs over, the one named last changes fastest.
Arguments:
- leaf_sol: bfloat16 [8, 256, 256], P(('layer', 'col'), 'row'), may hold values from -6 to 6
- lower_blocks: bfloat16 [8192, 1024], P(('layer', 'row'), 'col'), may hold values from -0.1875 to 0.1875
- lower_mask: int32 [32, 4], P(('layer', 'row'), 'col'), may hold values 0 or 1
- upper_blocks: bfloat16 [2048, 4096], P(('layer', 'col'), 'row'), may hold values from -0.125 to 0.125
- upper_mask: int32 [8, 16], P(('layer', 'col'), 'row'), may hold values 0 or 1
- anc_rhs: bfloat16 [4096, 256], P(('row', 'col')), may hold values from -6 to 6
- diag_inv: bfloat16 [4096, 256], P(('row', 'col')), may hold values from -0.375 to 0.375
Outputs:
- new_leaves: bfloat16 [8, 256, 256], P(('layer', 'col'), 'row')
- anc_sol: bfloat16 [4096, 256], P(('row', 'col'))
Inputs may be any that keep to these rules, and one draw needn't show every extreme that they name: `lower_mask`: 1 marks a stored block of L. `upper_mask`: 1 marks a stored block of U.
All inputs are finite; a program needn't handle non-finite values.
Results may differ from a plain program's by a relative error of at most 0.0044.
Values may be sent and summed in bfloat16 or wider, within the bound.
A program may use at most 64 MiB of HBM per device.

v0:
```python
import jax
import jax.numpy as jnp
from jax import lax
from jax.sharding import PartitionSpec as P


def expand(mask, block):
    first, second = mask.shape
    full = jnp.broadcast_to(mask[:, None, :, None], (first, block, second, block))
    return full.reshape(first * block, second * block)


def shards(leaf_sol, lower_blocks, lower_mask, upper_blocks, upper_mask, anc_rhs, diag_inv):
    block = diag_inv.shape[1]
    width = leaf_sol.shape[2]
    lower_masked = lower_blocks * expand(lower_mask, block).astype(jnp.bfloat16)
    upper_masked = upper_blocks * expand(upper_mask, block).astype(jnp.bfloat16)
    columns = lower_masked
    term = lax.dot_general(
        lax.all_gather(leaf_sol, "row", axis=1, tiled=True)[0],
        columns,
        (((0,), (1,)), ((), ())),
        preferred_element_type=jnp.float32,
    )
    inverse = diag_inv.astype(jnp.float32)
    layers = lax.axis_size("layer")
    columns = lax.axis_size("col")
    slice_width = width // layers
    pieces = term.reshape(layers, slice_width, columns, block)
    pieces = pieces.transpose(0, 2, 1, 3).reshape(layers * columns, slice_width, block)
    summed = lax.psum_scatter(pieces, ("layer", "col"), scatter_dimension=0, tiled=True)[0]
    layer_index = lax.axis_index("layer")
    rhs_part = lax.dynamic_slice_in_dim(anc_rhs, layer_index * slice_width, slice_width, 1)
    remain = rhs_part.astype(jnp.float32).T - summed
    solved_part = lax.dot_general(
        remain,
        inverse,
        (((1,), (1,)), ((), ())),
        precision=lax.Precision.HIGHEST,
        preferred_element_type=jnp.float32,
    ).astype(jnp.bfloat16)
    gathered_sides = lax.all_gather(solved_part, "layer", axis=0, tiled=True)
    anc_sol = gathered_sides.T
    columns = upper_masked
    folded = jnp.dot(
        columns,
        lax.all_gather(anc_sol, "col", axis=0, tiled=True),
        preferred_element_type=jnp.float32,
    )
    correct = lax.psum_scatter(folded, "row", scatter_dimension=0, tiled=True)
    new_leaves = (leaf_sol[0].astype(jnp.float32) - correct).astype(jnp.bfloat16)
    return (new_leaves.reshape(leaf_sol.shape), anc_sol)


def solution(mesh):
    in_specs = (
        P(("layer", "col"), "row", None),
        P(("layer", "row"), "col"),
        P(("layer", "row"), "col"),
        P(("layer", "col"), "row"),
        P(("layer", "col"), "row"),
        P(("row", "col"), None),
        P(("row", "col"), None),
    )
    out_specs = (P(("layer", "col"), "row", None), P(("row", "col"), None))
    return jax.shard_map(shards, mesh=mesh, in_specs=in_specs, out_specs=out_specs, check_vma=False)
```

profile of v0, /device:TPU:0, one launch (start us, length us, event | category | flops | bytes accessed | tf_op | source)
XLA Modules:
  0.0 106.7 jit_solution(17108516704674506642)
XLA Ops:
  7.2 0.0 copy-start
  7.2 0.0 reduce-scatter.3.cloned.1.call-start
  7.2 0.7 convert_bitcast_fusion
  7.9 0.1 broadcast_bitcast_fusion
  8.0 15.3 %all_gather.9 = bf16[1,256,256]{2,1,0:T(8,128)(2,1)S(1)} all-gather(bf16[1,64,256]{2,1,0:T(8,128)(2,1)} %param.7), channel_id=1, replica_groups=mesh['layer'=2,'row'=4,'col'=4] {'row'}, dimensions={1}, use_global_device_ids=true | all-gather | bytes 163840 | tf_op jit(solution)/shard_map/all_gather | solution.py:20
  23.3 1.4 %convolution_bitcast_fusion = f32[256,1024]{0,1:T(8,128)S(1)} fusion(bf16[1024,256]{1,0:T(8,128)(2,1)} %param.8, bf16[1024]{0:T(1024)(128)(2,1)S(1)} %bitcast.40, bf16[1,256,256]{2,1,0:T(8,128)(2,1)S(1)} %all_gather.9), kind=kOutput, calls=%fused_computation | convolution fusion | flops 134479872 | bytes 1705984 | tf_op jit(solution)/shard_map/dot_general | solution.py:19
  24.7 0.5 reshape.29
  25.2 1.0 copy.9
  26.3 0.0 copy-start.3
  26.3 0.0 reduce-scatter.3.cloned.1.call-update
  26.3 0.0 reduce-scatter.5.cloned.1.call-start
  26.4 0.0 copy-start.4
  26.4 0.6 copy-done.4
  27.0 0.1 broadcast_bitcast_fusion.1
  27.1 36.6 %reduce-scatter.3.cloned.1.call-done = f32[1,128,256]{1,2,0:T(8,128)} async-done(((f32[8,128,256]{1,2,0:T(8,128)}), f32[1,128,256]{1,2,0:T(8,128)}) %reduce-scatter.3.cloned.1.call-update) | async-done | bytes 131088 | tf_op jit(solution)/shard_map/reduce_scatter | solution.py:31
  63.7 0.0 copy-done
  63.7 0.0 copy-done.3
  63.7 1.2 %convolution_convert_fusion = bf16[128,256]{1,0:T(8,128)(2,1)S(1)} fusion(bf16[256,256]{1,0:T(8,128)(2,1)S(1)} %copy-done, f32[1,128,256]{1,2,0:T(8,128)} %reduce-scatter.3.cloned.1.call-done, bf16[256,256]{1,0:T(8,128)(2,1)S(1)} %copy-done.3, s32[]{:T(128)S(6)} %select_n.3), kind=kOutput, calls=%fused_computation.1 | convolution fusion | flops 100761600 | bytes 393220 | tf_op jit(solution)/shard_map/dot_general | solution.py:35
  65.0 0.0 copy-start.1
  65.0 5.1 %all_gather.10 = bf16[256,256]{1,0:T(8,128)(2,1)S(1)} all-gather(bf16[128,256]{1,0:T(8,128)(2,1)S(1)} %convolution_convert_fusion), channel_id=1, replica_groups=mesh['layer'=2,'row'=4,'col'=4] {'layer'}, dimensions={0}, use_global_device_ids=true | all-gather | bytes 196608 | tf_op jit(solution)/shard_map/all_gather | solution.py:42
  70.0 7.1 %all_gather.11 = bf16[1024,256]{0,1:T(8,128)(2,1)S(1)} all-gather(bf16[256,256]{0,1:T(8,128)(2,1)S(1)} %bitcast.37), channel_id=1, replica_groups=mesh['layer'=2,'row'=4,'col'=4] {'col'}, dimensions={0}, use_global_device_ids=true | all-gather | bytes 655360 | tf_op jit(solution)/shard_map/all_gather | solution.py:47
  77.2 0.0 copy-done.1
  77.2 1.0 fusion.1
  78.2 0.0 reduce-scatter.5.cloned.1.call-update
  78.2 0.0 copy-start.2
  78.2 0.8 copy.10
  79.0 19.4 %reduce-scatter.5.cloned.1.call-done = f32[64,256]{1,0:T(8,128)} async-done(((f32[256,256]{1,0:T(8,128)}), f32[64,256]{1,0:T(8,128)}) %reduce-scatter.5.cloned.1.call-update) | async-done | bytes 65552 | tf_op jit(solution)/shard_map/reduce_scatter | solution.py:50
  98.4 0.0 copy-done.2
  98.4 1.5 %fusion.10 = bf16[1,64,256]{2,1,0:T(8,128)(2,1)} fusion(f32[64,256]{1,0:T(8,128)} %reduce-scatter.5.cloned.1.call-done, bf16[1,64,256]{2,1,0:T(8,128)(2,1)S(1)} %copy-done.2), kind=kLoop, calls=%fused_computation.14 | loop fusion | flops 49152 | bytes 131072 | tf_op jit(solution)/shard_map/reshape | solution.py:52
  (3 shorter events, 0.0 us)
Async XLA Ops:
  7.2 56.6 %copy-start = (bf16[256,256]{1,0:T(8,128)(2,1)S(1)}, bf16[256,256]{1,0:T(8,128)(2,1)}, u32[]{:S(2)}) copy-start(bf16[256,256]{1,0:T(8,128)(2,1)} %param.13) | copy-start | bytes 393220
  7.2 56.6 %reduce-scatter.3.cloned.1.call-start = ((), (), s32[]{:S(2)}) async-start(), calls=%async_computation.2 | async-start | bytes 1179648 | tf_op jit(solution)/shard_map/reduce_scatter | solution.py:31
  26.3 37.5 %copy-start.3 = (bf16[256,256]{1,0:T(8,128)(2,1)S(1)}, bf16[256,256]{1,0:T(8,128)(2,1)}, u32[]{:S(2)}) copy-start(bf16[256,256]{1,0:T(8,128)(2,1)} %param.12) | copy-start | bytes 393220
  26.3 72.1 %reduce-scatter.5.cloned.1.call-start = ((), (), s32[]{:S(2)}) async-start(), calls=%async_computation.3 | async-start | bytes 327680 | tf_op jit(solution)/shard_map/reduce_scatter | solution.py:50
  26.4 0.7 copy-start.4
  65.0 12.2 %copy-start.1 = (bf16[256,1024]{1,0:T(8,128)(2,1)S(1)}, bf16[256,1024]{1,0:T(8,128)(2,1)}, u32[]{:S(2)}) copy-start(bf16[256,1024]{1,0:T(8,128)(2,1)} %param.10) | copy-start | bytes 1572868
  78.2 20.1 %copy-start.2 = (bf16[1,64,256]{2,1,0:T(8,128)(2,1)S(1)}, bf16[1,64,256]{2,1,0:T(8,128)(2,1)}, u32[]{:S(2)}) copy-start(bf16[1,64,256]{2,1,0:T(8,128)(2,1)} %param.7) | copy-start | bytes 98308
Sparse Core Ops, SparseCore 0:
  26.4 37.2 reduce-scatter.2
  78.3 19.9 reduce-scatter.4
where the time goes:
time: 107 us
  waiting for transfers between devices  56 us (52%)
  blocking collectives  27.5 us (26%)
  between operations  14.1 us (13%)
  matrix products  3.63 us (3%)
  local copies, waits for them, and re-layouts  3.19 us (3%)
  other arithmetic  2.15 us (2%)
    reduce_scatter x1, waiting for transfers between devices, shards(): lax.psum_scatter(pieces, ('layer', 'col'), scatter_dimension=0, tiled=True)  36.6 us
    reduce_scatter x1, waiting for transfers between devices, shards(): correct = lax.psum_scatter(folded, 'row', scatter_dimension=0, tiled=True)  19.4 us
    all_gather x1, blocking collectives, shards(): lax.all_gather(leaf_sol, 'row', axis=1, tiled=True)[0]  15.3 us
    all_gather x1, blocking collectives, shards(): lax.all_gather(anc_sol, 'col', axis=0, tiled=True)  7.13 us
    all_gather x1, blocking collectives, shards(): gathered_sides = lax.all_gather(solved_part, 'layer', axis=0, tiled=True)  5.07 us
  transfers between devices with their start and end apart: 2, of which 2 were waited for; matrix products, arithmetic and copies ran while one was open for 1% of the time, Pallas kernels for 0%

commit v1 on v0

v1 whole, which is shorter than its diff:
```python
import functools

import jax
import jax.numpy as jnp
from jax import lax
from jax.experimental import pallas as pl
from jax.experimental.pallas import tpu as pltpu
from jax.sharding import PartitionSpec as P

MESH = pl.DeviceIdType.MESH


def dot_last(a, b):
    return lax.dot_general(a, b, (((1,), (1,)), ((), ())), preferred_element_type=jnp.float32)


def kernel(
    n_layer, n_row, n_col,
    leaf, lower, lower_mask, upper, upper_mask, rhs, inv,
    new_leaves, anc_out,
    leaf_v, lower_v, upper_v, rhs_v, inv_v, x_all, x_t, rhs_t, part, part_in, anc_t, fold, fold_in,
    local_sem, x_send, x_recv, part_send, part_recv, anc_send, anc_recv, fold_send, fold_recv,
):
    layer = lax.axis_index("layer")
    row = lax.axis_index("row")
    col = lax.axis_index("col")
    block = inv_v.shape[0]
    width = rhs_v.shape[1]
    share = width // n_layer
    strip = leaf_v.shape[0]
    depth = x_all.shape[0] * strip
    group = [(dl, dc) for dl in range(n_layer) for dc in range(n_col) if (dl, dc) != (0, 0)]

    loads = [
        pltpu.make_async_copy(source, target, local_sem.at[index])
        for index, (source, target) in enumerate(
            ((leaf.at[0], leaf_v), (lower, lower_v), (rhs, rhs_v), (inv, inv_v), (upper, upper_v))
        )
    ]
    for load in loads:
        load.start()

    barrier = pltpu.get_barrier_semaphore()
    for dr in range(1, n_row):
        pl.semaphore_signal(barrier, inc=1, device_id=(layer, lax.rem(row + dr, n_row), col), device_id_type=MESH)
    for dl, dc in group:
        pl.semaphore_signal(
            barrier, inc=1,
            device_id=(lax.rem(layer + dl, n_layer), row, lax.rem(col + dc, n_col)), device_id_type=MESH,
        )
    pl.semaphore_wait(barrier, n_row - 1 + len(group))

    def x_copy(to_row, from_row):
        return pltpu.make_async_remote_copy(
            src_ref=leaf.at[0], dst_ref=x_all.at[from_row],
            send_sem=x_send.at[to_row], recv_sem=x_recv.at[from_row],
            device_id=(layer, to_row, col), device_id_type=MESH,
        )

    for dr in range(1, n_row):
        x_copy(lax.rem(row + dr, n_row), row).start()
    loads[0].wait()
    x_all[row] = leaf_v[...]
    loads[2].wait()
    rhs_t[...] = rhs_v[...].astype(jnp.float32).T
    loads[1].wait()
    loads[3].wait()
    for dr in range(1, n_row):
        x_copy(row, lax.rem(row + dr, n_row)).wait_recv()
    for k in range(depth // block):
        strips = block // strip
        x_t[k] = x_all[k * strips:(k + 1) * strips].reshape(block, width).T

    def part_copy(source, to_layer, to_col, from_layer, from_col):
        return pltpu.make_async_remote_copy(
            src_ref=source, dst_ref=part_in.at[from_layer * n_col + from_col],
            send_sem=part_send.at[to_layer * n_col + to_col],
            recv_sem=part_recv.at[from_layer * n_col + from_col],
            device_id=(to_layer, row, to_col), device_id_type=MESH,
        )

    own = None
    for dc in list(range(1, n_col)) + [0]:
        to_col = lax.rem(col + dc, n_col)
        total = None
        for k in range(depth // block):
            rows = lower_v[pl.ds(pl.multiple_of(to_col * block, block), block), k * block:(k + 1) * block]
            term = dot_last(x_t[k], rows) * lower_mask[k, to_col].astype(jnp.float32)
            total = term if total is None else total + term
        part[to_col] = total.astype(jnp.bfloat16)
        for dl in list(range(1, n_layer)) + [0]:
            to_layer = lax.rem(layer + dl, n_layer)
            if (dl, dc) != (0, 0):
                part_copy(
                    part.at[to_col, pl.ds(pl.multiple_of(to_layer * share, share), share)],
                    to_layer, to_col, layer, col,
                ).start()

    mine = pl.ds(pl.multiple_of(layer * share, share), share)
    remain = rhs_t[mine, :] - part[col, mine, :].astype(jnp.float32)
    for dl, dc in group:
        from_layer, from_col = lax.rem(layer + dl, n_layer), lax.rem(col + dc, n_col)
        part_copy(part.at[0, pl.ds(0, share)], layer, col, from_layer, from_col).wait_recv()
        remain = remain - part_in[from_layer * n_col + from_col].astype(jnp.float32)
    inverse = inv_v[...]
    high = remain.astype(jnp.bfloat16)
    rest = remain - high.astype(jnp.float32)
    middle = rest.astype(jnp.bfloat16)
    low = (rest - middle.astype(jnp.float32)).astype(jnp.bfloat16)
    solved = dot_last(high, inverse) + (dot_last(middle, inverse) + dot_last(low, inverse))
    anc_t[col, mine, :] = solved.astype(jnp.bfloat16)

    def anc_copy(to_layer, to_col, from_layer, from_col):
        place = anc_t.at[from_col, pl.ds(pl.multiple_of(from_layer * share, share), share)]
        return pltpu.make_async_remote_copy(
            src_ref=place, dst_ref=place,
            send_sem=anc_send.at[to_layer * n_col + to_col],
            recv_sem=anc_recv.at[from_layer * n_col + from_col],
            device_id=(to_layer, row, to_col), device_id_type=MESH,
        )

    for dl, dc in reversed(group):
        anc_copy(lax.rem(layer + dl, n_layer), lax.rem(col + dc, n_col), layer, col).start()

    loads[4].wait()
    blocks_down = upper_v.shape[0] // block
    totals = [None] * blocks_down
    for dc in range(n_col):
        from_col = lax.rem(col + dc, n_col)
        for dl in range(n_layer):
            if (dl, dc) != (0, 0):
                anc_copy(layer, col, lax.rem(layer + dl, n_layer), from_col).wait_recv()
        for i in range(blocks_down):
            tile = upper_v[i * block:(i + 1) * block, pl.ds(pl.multiple_of(from_col * block, block), block)]
            term = dot_last(tile, anc_t[from_col]) * upper_mask[i, from_col].astype(jnp.float32)
            totals[i] = term if totals[i] is None else totals[i] + term
    strips = block // strip
    for i in range(blocks_down):
        fold[i * strips:(i + 1) * strips] = totals[i].astype(jnp.bfloat16).reshape(strips, strip, width)

    def fold_copy(to_row, from_row):
        return pltpu.make_async_remote_copy(
            src_ref=fold.at[to_row], dst_ref=fold_in.at[from_row],
            send_sem=fold_send.at[to_row], recv_sem=fold_recv.at[from_row],
            device_id=(layer, to_row, col), device_id_type=MESH,
        )

    for dr in range(1, n_row):
        fold_copy(lax.rem(row + dr, n_row), row).start()
    anc_out[...] = anc_t[col].T
    correct = fold[row].astype(jnp.float32)
    for dr in range(1, n_row):
        from_row = lax.rem(row + dr, n_row)
        fold_copy(row, from_row).wait_recv()
        correct = correct + fold_in[from_row].astype(jnp.float32)
    new_leaves[0] = (leaf_v[...].astype(jnp.float32) - correct).astype(jnp.bfloat16)

    for dr in range(1, n_row):
        x_copy(lax.rem(row + dr, n_row), row).wait_send()
        fold_copy(lax.rem(row + dr, n_row), row).wait_send()
    for dl, dc in group:
        to_layer, to_col = lax.rem(layer + dl, n_layer), lax.rem(col + dc, n_col)
        part_copy(part.at[0, pl.ds(0, share)], to_layer, to_col, layer, col).wait_send()
        anc_copy(to_layer, to_col, layer, col).wait_send()


def shards(n_layer, n_row, n_col, leaf_sol, lower_blocks, lower_mask, upper_blocks, upper_mask, anc_rhs, diag_inv):
    block = diag_inv.shape[1]
    width = leaf_sol.shape[2]
    strip = leaf_sol.shape[1]
    share = width // n_layer
    bf16 = jnp.bfloat16
    dma = pltpu.SemaphoreType.DMA
    anywhere = pl.BlockSpec(memory_space=pl.ANY)
    scalars = pl.BlockSpec(memory_space=pltpu.SMEM)
    vmem = pl.BlockSpec(memory_space=pltpu.VMEM)
    devices = n_layer * n_col
    return pl.pallas_call(
        functools.partial(kernel, n_layer, n_row, n_col),
        out_shape=(
            jax.ShapeDtypeStruct(leaf_sol.shape, bf16),
            jax.ShapeDtypeStruct(anc_rhs.shape, bf16),
        ),
        in_specs=[anywhere, anywhere, scalars, anywhere, scalars, anywhere, anywhere],
        out_specs=(vmem, vmem),
        scratch_shapes=[
            pltpu.VMEM((strip, width), bf16),
            pltpu.VMEM(lower_blocks.shape, bf16),
            pltpu.VMEM(upper_blocks.shape, bf16),
            pltpu.VMEM(anc_rhs.shape, bf16),
            pltpu.VMEM(diag_inv.shape, bf16),
            pltpu.VMEM((n_row, strip, width), bf16),
            pltpu.VMEM((n_row * strip // block, width, block), bf16),
            pltpu.VMEM((width, block), jnp.float32),
            pltpu.VMEM((n_col, width, block), bf16),
            pltpu.VMEM((devices, share, block), bf16),
            pltpu.VMEM((n_col, width, block), bf16),
            pltpu.VMEM((n_row, strip, width), bf16),
            pltpu.VMEM((n_row, strip, width), bf16),
            dma((5,)),
            dma((n_row,)), dma((n_row,)),
            dma((devices,)), dma((devices,)),
            dma((devices,)), dma((devices,)),
            dma((n_row,)), dma((n_row,)),
        ],
        compiler_params=pltpu.CompilerParams(collective_id=0, has_side_effects=True),
    )(leaf_sol, lower_blocks, lower_mask.T, upper_blocks, upper_mask, anc_rhs, diag_inv)


def solution(mesh):
    in_specs = (
        P(("layer", "col"), "row", None),
        P(("layer", "row"), "col"),
        P(("layer", "row"), "col"),
        P(("layer", "col"), "row"),
        P(("layer", "col"), "row"),
        P(("row", "col"), None),
        P(("row", "col"), None),
    )
    out_specs = (P(("layer", "col"), "row", None), P(("row", "col"), None))
    body = functools.partial(shards, mesh.shape["layer"], mesh.shape["row"], mesh.shape["col"])
    return jax.shard_map(body, mesh=mesh, in_specs=in_specs, out_specs=out_specs, check_vma=False)
```

time: 107 us -> 35.7 us (0.33)
  waiting for transfers between devices: 56 us -> 0 us
  Pallas kernels: 0 us -> 31.9 us
  blocking collectives: 27.5 us -> 0 us
  between operations: 14.1 us -> 0.64 us
  matrix products: 3.63 us -> 0 us
  other arithmetic: 2.15 us -> 0 us
    reduce_scatter x2 -> x0, waiting for transfers between devices: 56 us -> none  [the longest x1 36.6 us: shards(): lax.psum_scatter(pieces, ('layer', 'col'), scatter_dimension=0, tiled=True)]
    pallas_call x0 -> x1, Pallas kernels: none -> 31.9 us  [shards(): pl.pallas_call(functools.partial(kernel, n_layer, n_row, n_col), out_shap...]
    all_gather x3 -> x0, blocking collectives: 27.5 us -> none  [the longest x1 15.3 us: shards(): lax.all_gather(leaf_sol, 'row', axis=1, tiled=True)[0]]
    dot_general x3 -> x0, matrix products: 3.63 us -> none  [the longest x1 1.39 us: shards(): lax.dot_general(lax.all_gather(leaf_sol, 'row', axis=1, tiled=True)[0], c...]
    reshape x1 -> x0, other arithmetic: 1.46 us -> none  [shards(): return (new_leaves.reshape(leaf_sol.shape), anc_sol)]
    unnamed x15 -> x2, local copies, waits for them, and re-layouts: 1.6 us -> 2.94 us
  transfers between devices with their start and end apart: 2 -> 0, of which waited for: 2 -> 0; matrix products, arithmetic and copies ran while one was open for 1% -> 0% of each run, Pallas kernels for 0% -> 0%
where the time goes in v1:
time: 35.7 us; the launch traced here: 35.5 us
  Pallas kernels  31.9 us (89%)
  local copies, waits for them, and re-layouts  2.94 us (8%)
  between operations  0.64 us (2%)
    pallas_call x1, Pallas kernels, shards(): pl.pallas_call(functools.partial(kernel, n_layer, n_row, n_col), out_shap...  31.9 us
    unnamed x2, local copies, waits for them, and re-layouts  2.94 us

profile of v1, /device:TPU:0, one launch (start us, length us, event | category | flops | bytes accessed | tf_op | source)
XLA Modules:
  0.0 35.5 jit_solution(8851827594193969914)
XLA Ops:
  0.6 31.9 %shard_map.86 = (bf16[1,64,256]{2,1,0:T(8,128)(2,1)}, bf16[256,256]{1,0:T(8,128)(2,1)}) custom-call(bf16[1,64,256]{2,1,0:T(8,128)(2,1)} %leaf.1, bf16[1024,256]{1,0:T(8,128)(2,1)} %lower.1, s32[1,4]{1,0:T(1,128)} %bitcast.1, bf16[256,1024]{1,0:T(8,128)(2,1)} %upper.1, s32[1,4]{1,0:T(1,128)} %upper_mask.1, bf16[256,256]{1,0:T(8,128)(2,1)} %rhs.1, ...), custom_call_target="tpu_custom_call" | custom-call | tf_op jit(solution)/shard_map/pallas_call | solution.py:178
  32.5 1.4 %copy.11 = bf16[1,64,256]{2,1,0:T(8,128)(2,1)} copy(bf16[1,64,256]{2,1,0:T(8,128)(2,1)} %get-tuple-element.4) | data formatting | bytes 65536
  33.9 1.6 %copy.12 = bf16[256,256]{1,0:T(8,128)(2,1)} copy(bf16[256,256]{1,0:T(8,128)(2,1)} %get-tuple-element.5) | data formatting | bytes 262144

commit v2 on v1

v2 whole, which is shorter than its diff:
```python
import functools

import jax
import jax.numpy as jnp
from jax import lax
from jax.experimental import pallas as pl
from jax.experimental.pallas import tpu as pltpu
from jax.sharding import PartitionSpec as P

MESH = pl.DeviceIdType.MESH


def dot_last(a, b):
    return lax.dot_general(a, b, (((1,), (1,)), ((), ())), preferred_element_type=jnp.float32)


def kernel(
    n_layer, n_row, n_col, chunks,
    leaf, lower, lower_mask, upper, upper_mask, rhs, inv,
    new_leaves, anc_out,
    leaf_v, lower_v, upper_v, rhs_v, inv_v, x_all, x_t, rhs_t,
    pair_out, pair_in, held, part, part_in, anc_t, fold, fold_in,
    local_sem, x_send, x_recv, pair_send, pair_recv, part_send, part_recv,
    anc_send, pass_send, anc_recv, fold_send, fold_recv,
):
    layer = lax.axis_index("layer")
    row = lax.axis_index("row")
    col = lax.axis_index("col")
    halves = n_col // 2
    half, side = col // 2, lax.rem(col, 2)
    other = 1 - side
    partner = half * 2 + other
    block = inv_v.shape[0]
    width = rhs_v.shape[1]
    span = width // chunks
    share = span // n_layer
    strip = leaf_v.shape[0]
    depth = x_all.shape[0] * strip
    devices = n_layer * n_col
    group = [(dl, dh) for dl in range(n_layer) for dh in range(halves) if (dl, dh) != (0, 0)]

    def peer(dl, dh):
        return lax.rem(layer + dl, n_layer), lax.rem(half + dh, halves) * 2 + side

    loads = [
        pltpu.make_async_copy(source, target, local_sem.at[index])
        for index, (source, target) in enumerate(
            ((leaf.at[0], leaf_v), (lower, lower_v), (rhs, rhs_v), (inv, inv_v), (upper, upper_v))
        )
    ]
    for load in loads:
        load.start()

    barrier = pltpu.get_barrier_semaphore()
    for dr in reversed(range(1, n_row)):
        pl.semaphore_signal(barrier, inc=1, device_id=(layer, lax.rem(row + dr, n_row), col), device_id_type=MESH)
    for dl, dh in group:
        to_layer, to_col = peer(dl, dh)
        pl.semaphore_signal(barrier, inc=1, device_id=(to_layer, row, to_col), device_id_type=MESH)
    pl.semaphore_signal(barrier, inc=1, device_id=(layer, row, partner), device_id_type=MESH)
    pl.semaphore_wait(barrier, n_row + len(group))

    def x_copy(to_row, from_row):
        return pltpu.make_async_remote_copy(
            src_ref=leaf.at[0], dst_ref=x_all.at[from_row],
            send_sem=x_send.at[to_row], recv_sem=x_recv.at[from_row],
            device_id=(layer, to_row, col), device_id_type=MESH,
        )

    for dr in range(1, n_row):
        x_copy(lax.rem(row + dr, n_row), row).start()
    loads[0].wait()
    x_all[row] = leaf_v[...]
    loads[2].wait()
    rhs_t[...] = rhs_v[...].astype(jnp.float32).T
    loads[1].wait()
    loads[3].wait()
    loads[4].wait()
    for dr in range(1, n_row):
        x_copy(row, lax.rem(row + dr, n_row)).wait_recv()
    strips = block // strip
    for k in range(depth // block):
        x_t[k] = x_all[k * strips:(k + 1) * strips].reshape(block, width).T

    def partial_sum(j, to_col):
        total = None
        for k in range(depth // block):
            rows = lower_v[pl.ds(pl.multiple_of(to_col * block, block), block), k * block:(k + 1) * block]
            term = dot_last(x_t[k, j * span:(j + 1) * span], rows) * lower_mask[k, to_col].astype(jnp.float32)
            total = term if total is None else total + term
        return total

    def pair_copy(j, h):
        return pltpu.make_async_remote_copy(
            src_ref=pair_out.at[j, h], dst_ref=pair_in.at[j, h],
            send_sem=pair_send.at[j * halves + h], recv_sem=pair_recv.at[j * halves + h],
            device_id=(layer, row, partner), device_id_type=MESH,
        )

    for j in range(chunks):
        for h in range(halves):
            pair_out[j, h] = partial_sum(j, h * 2 + other).astype(jnp.bfloat16)
            pair_copy(j, h).start()
        for h in range(halves):
            held[j, h] = partial_sum(j, h * 2 + side)

    def inside(index):
        return pl.ds(pl.multiple_of(index * share, share), share)

    def part_copy(j, to_layer, to_col, from_layer, from_col):
        return pltpu.make_async_remote_copy(
            src_ref=part.at[j, to_col // 2, inside(to_layer)],
            dst_ref=part_in.at[j, from_layer * n_col + from_col],
            send_sem=part_send.at[j * devices + to_layer * n_col + to_col],
            recv_sem=part_recv.at[j * devices + from_layer * n_col + from_col],
            device_id=(to_layer, row, to_col), device_id_type=MESH,
        )

    for j in range(chunks):
        for h in range(halves):
            pair_copy(j, h).wait_recv()
            total = held[j, h] + pair_in[j, h].astype(jnp.float32)
            held[j, h] = total
            part[j, h] = total.astype(jnp.bfloat16)
        for dl, dh in reversed(group):
            part_copy(j, *peer(dl, dh), layer, col).start()

    def anc_place(j, from_layer, from_col):
        return anc_t.at[j, from_col, inside(from_layer)]

    def anc_copy(j, to_layer, to_col, from_layer, from_col):
        place = anc_place(j, from_layer, from_col)
        return pltpu.make_async_remote_copy(
            src_ref=place, dst_ref=place,
            send_sem=anc_send.at[j * devices + to_layer * n_col + to_col],
            recv_sem=anc_recv.at[j * devices + from_layer * n_col + from_col],
            device_id=(to_layer, row, to_col), device_id_type=MESH,
        )

    def pass_copy(j, from_layer, from_col):
        place = anc_place(j, from_layer, from_col)
        return pltpu.make_async_remote_copy(
            src_ref=place, dst_ref=place,
            send_sem=pass_send.at[j * devices + from_layer * n_col + from_col],
            recv_sem=anc_recv.at[j * devices + from_layer * n_col + from_col],
            device_id=(layer, row, partner), device_id_type=MESH,
        )

    inverse = inv_v[...]
    for j in range(chunks):
        remain = rhs_t[pl.ds(pl.multiple_of(j * span + layer * share, share), share), :] - held[j, half, inside(layer)]
        for dl, dh in group:
            from_layer, from_col = peer(dl, dh)
            part_copy(j, layer, col, from_layer, from_col).wait_recv()
            remain = remain - part_in[j, from_layer * n_col + from_col].astype(jnp.float32)
        high = remain.astype(jnp.bfloat16)
        rest = remain - high.astype(jnp.float32)
        middle = rest.astype(jnp.bfloat16)
        low = (rest - middle.astype(jnp.float32)).astype(jnp.bfloat16)
        solved = dot_last(high, inverse) + (dot_last(middle, inverse) + dot_last(low, inverse))
        anc_t[j, col, inside(layer)] = solved.astype(jnp.bfloat16)
        for dl, dh in reversed(group):
            anc_copy(j, *peer(dl, dh), layer, col).start()
        pass_copy(j, layer, col).start()

    def fold_copy(j, to_row, from_row):
        return pltpu.make_async_remote_copy(
            src_ref=fold.at[j, to_row], dst_ref=fold_in.at[j, from_row],
            send_sem=fold_send.at[j * n_row + to_row], recv_sem=fold_recv.at[j * n_row + from_row],
            device_id=(layer, to_row, col), device_id_type=MESH,
        )

    blocks_down = upper_v.shape[0] // block
    for j in range(chunks):
        for dl, dh in group:
            from_layer, from_col = peer(dl, dh)
            anc_copy(j, layer, col, from_layer, from_col).wait_recv()
            pass_copy(j, from_layer, from_col).start()
        totals = [None] * blocks_down
        for parity in (side, other):
            for dh in range(halves):
                from_col = lax.rem(half + dh, halves) * 2 + parity
                if parity is other:
                    for from_layer in range(n_layer):
                        pass_copy(j, from_layer, from_col).wait_recv()
                for i in range(blocks_down):
                    tile = upper_v[i * block:(i + 1) * block, pl.ds(pl.multiple_of(from_col * block, block), block)]
                    term = dot_last(tile, anc_t[j, from_col]) * upper_mask[i, from_col].astype(jnp.float32)
                    totals[i] = term if totals[i] is None else totals[i] + term
        for i in range(blocks_down):
            fold[j, i * strips:(i + 1) * strips] = totals[i].astype(jnp.bfloat16).reshape(strips, strip, span)
        for dr in range(1, n_row):
            fold_copy(j, lax.rem(row + dr, n_row), row).start()

    for j in range(chunks):
        anc_out[:, j * span:(j + 1) * span] = anc_t[j, col].T
    for j in range(chunks):
        correct = fold[j, row].astype(jnp.float32)
        for dr in range(1, n_row):
            from_row = lax.rem(row + dr, n_row)
            fold_copy(j, row, from_row).wait_recv()
            correct = correct + fold_in[j, from_row].astype(jnp.float32)
        columns = slice(j * span, (j + 1) * span)
        new_leaves[0, :, columns] = (leaf_v[:, columns].astype(jnp.float32) - correct).astype(jnp.bfloat16)

    for dr in range(1, n_row):
        x_copy(lax.rem(row + dr, n_row), row).wait_send()
        for j in range(chunks):
            fold_copy(j, lax.rem(row + dr, n_row), row).wait_send()
    for j in range(chunks):
        for h in range(halves):
            pair_copy(j, h).wait_send()
        pass_copy(j, layer, col).wait_send()
        for dl, dh in group:
            to_layer, to_col = peer(dl, dh)
            part_copy(j, to_layer, to_col, layer, col).wait_send()
            anc_copy(j, to_layer, to_col, layer, col).wait_send()
            pass_copy(j, to_layer, to_col).wait_send()


def finish(leaves, anc, leaves_out, anc_out):
    leaves_out[...] = leaves[...]
    anc_out[...] = anc[...]


def shards(n_layer, n_row, n_col, leaf_sol, lower_blocks, lower_mask, upper_blocks, upper_mask, anc_rhs, diag_inv):
    block = diag_inv.shape[1]
    width = leaf_sol.shape[2]
    strip = leaf_sol.shape[1]
    chunks = 2
    span = width // chunks
    share = span // n_layer
    halves = n_col // 2
    bf16, f32 = jnp.bfloat16, jnp.float32
    anywhere = pl.BlockSpec(memory_space=pltpu.HBM)
    scalars = pl.BlockSpec(memory_space=pltpu.SMEM)
    vmem = pl.BlockSpec(memory_space=pltpu.VMEM)
    devices = n_layer * n_col
    dma = lambda *sizes: [pltpu.SemaphoreType.DMA((size,)) for size in sizes]
    out_shape = (
        jax.ShapeDtypeStruct(leaf_sol.shape, bf16),
        jax.ShapeDtypeStruct(anc_rhs.shape, bf16),
    )
    results = pl.pallas_call(
        functools.partial(kernel, n_layer, n_row, n_col, chunks),
        out_shape=out_shape,
        in_specs=[anywhere, anywhere, scalars, anywhere, scalars, anywhere, anywhere],
        out_specs=(vmem, vmem),
        scratch_shapes=[
            pltpu.VMEM((strip, width), bf16),
            pltpu.VMEM(lower_blocks.shape, bf16),
            pltpu.VMEM(upper_blocks.shape, bf16),
            pltpu.VMEM(anc_rhs.shape, bf16),
            pltpu.VMEM(diag_inv.shape, bf16),
            pltpu.VMEM((n_row, strip, width), bf16),
            pltpu.VMEM((n_row * strip // block, width, block), bf16),
            pltpu.VMEM((width, block), f32),
            pltpu.VMEM((chunks, halves, span, block), bf16),
            pltpu.VMEM((chunks, halves, span, block), bf16),
            pltpu.VMEM((chunks, halves, span, block), f32),
            pltpu.VMEM((chunks, halves, span, block), bf16),
            pltpu.VMEM((chunks, devices, share, block), bf16),
            pltpu.VMEM((chunks, n_col, span, block), bf16),
            pltpu.VMEM((chunks, n_row, strip, span), bf16),
            pltpu.VMEM((chunks, n_row, strip, span), bf16),
            *dma(
                5, n_row, n_row, chunks * halves, chunks * halves,
                *[chunks * devices] * 5, chunks * n_row, chunks * n_row,
            ),
        ],
        compiler_params=pltpu.CompilerParams(
            collective_id=0, has_side_effects=True,
        ),
    )(leaf_sol, lower_blocks, lower_mask.T, upper_blocks, upper_mask, anc_rhs, diag_inv)
    return pl.pallas_call(finish, out_shape=out_shape, in_specs=[vmem] * 2, out_specs=(vmem, vmem))(*results)


def solution(mesh):
    in_specs = (
        P(("layer", "col"), "row", None),
        P(("layer", "row"), "col"),
        P(("layer", "row"), "col"),
        P(("layer", "col"), "row"),
        P(("layer", "col"), "row"),
        P(("row", "col"), None),
        P(("row", "col"), None),
    )
    out_specs = (P(("layer", "col"), "row", None), P(("row", "col"), None))
    body = functools.partial(shards, mesh.shape["layer"], mesh.shape["row"], mesh.shape["col"])
    return jax.shard_map(body, mesh=mesh, in_specs=in_specs, out_specs=out_specs, check_vma=False)
```

time: 35.7 us -> 31.8 us (0.89)
  local copies, waits for them, and re-layouts: 2.94 us -> 0 us
  Pallas kernels: 31.9 us -> 31 us
    unnamed x2 -> x0, local copies, waits for them, and re-layouts: 2.94 us -> none
    pallas_call x1 -> x2, Pallas kernels: 31.9 us -> 31 us  [the longest x1 29.4 us: shards(): pl.pallas_call(functools.partial(kernel, n_layer, n_row, n_col, chunks),...]
where the time goes in v2:
time: 31.8 us; the launch traced here: 31.6 us
  Pallas kernels  31 us (97%)
  between operations  0.64 us (2%)
    pallas_call x1, Pallas kernels, shards(): pl.pallas_call(functools.partial(kernel, n_layer, n_row, n_col, chunks),...  29.4 us
    pallas_call x1, Pallas kernels, shards(): pl.pallas_call(finish, out_shape=out_shape, in_specs=[vmem] * 2, out_spec...  1.59 us

profile of v2, /device:TPU:0, one launch (start us, length us, event | category | flops | bytes accessed | tf_op | source)
XLA Modules:
  0.0 31.6 jit_solution(14007405269197660260)
XLA Ops:
  0.6 29.4 %shard_map.86 = (bf16[1,64,256]{2,1,0:T(8,128)(2,1)}, bf16[256,256]{1,0:T(8,128)(2,1)}) custom-call(bf16[1,64,256]{2,1,0:T(8,128)(2,1)} %leaf.1, bf16[1024,256]{1,0:T(8,128)(2,1)} %lower.1, s32[1,4]{1,0:T(1,128)} %bitcast.1, bf16[256,1024]{1,0:T(8,128)(2,1)} %upper.1, s32[1,4]{1,0:T(1,128)} %upper_mask.1, bf16[256,256]{1,0:T(8,128)(2,1)} %rhs.1, ...), custom_call_target="tpu_custom_call" | custom-call | tf_op jit(solution)/shard_map/pallas_call | solution.py:244
  30.0 1.6 %shard_map.87 = (bf16[1,64,256]{2,1,0:T(8,128)(2,1)}, bf16[256,256]{1,0:T(8,128)(2,1)}) custom-call(bf16[1,64,256]{2,1,0:T(8,128)(2,1)} %get-tuple-element.4.leaves, bf16[256,256]{1,0:T(8,128)(2,1)} %get-tuple-element.5.anc), custom_call_target="tpu_custom_call" | custom-call | tf_op jit(solution)/shard_map/pallas_call | solution.py:275

commit v3 on v2

--- a/solution.py
+++ b/solution.py
@@ -35,7 +35,7 @@
     span = width // chunks
     share = span // n_layer
     strip = leaf_v.shape[0]
-    depth = x_all.shape[0] * strip
+    depth = n_row * strip
     devices = n_layer * n_col
     group = [(dl, dh) for dl in range(n_layer) for dh in range(halves) if (dl, dh) != (0, 0)]
 
@@ -60,33 +60,31 @@
     pl.semaphore_signal(barrier, inc=1, device_id=(layer, row, partner), device_id_type=MESH)
     pl.semaphore_wait(barrier, n_row + len(group))
 
-    def x_copy(to_row, from_row):
-        return pltpu.make_async_remote_copy(
-            src_ref=leaf.at[0], dst_ref=x_all.at[from_row],
-            send_sem=x_send.at[to_row], recv_sem=x_recv.at[from_row],
+    def x_copy(j, to_row, from_row):
+        return pltpu.make_async_remote_copy(
+            src_ref=leaf.at[0, :, pl.ds(j * span, span)], dst_ref=x_all.at[j, from_row],
+            send_sem=x_send.at[j * n_row + to_row], recv_sem=x_recv.at[j * n_row + from_row],
             device_id=(layer, to_row, col), device_id_type=MESH,
         )
 
-    for dr in range(1, n_row):
-        x_copy(lax.rem(row + dr, n_row), row).start()
+    for j in range(chunks):
+        for dr in range(1, n_row):
+            x_copy(j, lax.rem(row + dr, n_row), row).start()
     loads[0].wait()
-    x_all[row] = leaf_v[...]
+    for j in range(chunks):
+        x_all[j, row] = leaf_v[:, j * span:(j + 1) * span]
     loads[2].wait()
     rhs_t[...] = rhs_v[...].astype(jnp.float32).T
     loads[1].wait()
     loads[3].wait()
     loads[4].wait()
-    for dr in range(1, n_row):
-        x_copy(row, lax.rem(row + dr, n_row)).wait_recv()
     strips = block // strip
-    for k in range(depth // block):
-        x_t[k] = x_all[k * strips:(k + 1) * strips].reshape(block, width).T
 
     def partial_sum(j, to_col):
         total = None
         for k in range(depth // block):
             rows = lower_v[pl.ds(pl.multiple_of(to_col * block, block), block), k * block:(k + 1) * block]
-            term = dot_last(x_t[k, j * span:(j + 1) * span], rows) * lower_mask[k, to_col].astype(jnp.float32)
+            term = dot_last(x_t[j, k], rows) * lower_mask[k, to_col].astype(jnp.float32)
             total = term if total is None else total + term
         return total
 
@@ -97,26 +95,28 @@
             device_id=(layer, row, partner), device_id_type=MESH,
         )
 
-    for j in range(chunks):
+    def inside(index):
+        return pl.ds(pl.multiple_of(index * share, share), share)
+
+    def part_copy(j, to_layer, to_col, from_layer, from_col):
+        return pltpu.make_async_remote_copy(
+            src_ref=part.at[j, to_col // 2, inside(to_layer)],
+            dst_ref=part_in.at[j, from_layer * n_col + from_col],
+            send_sem=part_send.at[j * devices + to_layer * n_col + to_col],
+            recv_sem=part_recv.at[j * devices + from_layer * n_col + from_col],
+            device_id=(to_layer, row, to_col), device_id_type=MESH,
+        )
+
+    for j in range(chunks):
+        for dr in range(1, n_row):
+            x_copy(j, row, lax.rem(row + dr, n_row)).wait_recv()
+        for k in range(depth // block):
+            x_t[j, k] = x_all[j, k * strips:(k + 1) * strips].reshape(block, span).T
         for h in range(halves):
             pair_out[j, h] = partial_sum(j, h * 2 + other).astype(jnp.bfloat16)
             pair_copy(j, h).start()
         for h in range(halves):
             held[j, h] = partial_sum(j, h * 2 + side)
-
-    def inside(index):
-        return pl.ds(pl.multiple_of(index * share, share), share)
-
-    def part_copy(j, to_layer, to_col, from_layer, from_col):
-        return pltpu.make_async_remote_copy(
-            src_ref=part.at[j, to_col // 2, inside(to_layer)],
-            dst_ref=part_in.at[j, from_layer * n_col + from_col],
-            send_sem=part_send.at[j * devices + to_layer * n_col + to_col],
-            recv_sem=part_recv.at[j * devices + from_layer * n_col + from_col],
-            device_id=(to_layer, row, to_col), device_id_type=MESH,
-        )
-
-    for j in range(chunks):
         for h in range(halves):
             pair_copy(j, h).wait_recv()
             total = held[j, h] + pair_in[j, h].astype(jnp.float32)
@@ -204,8 +204,8 @@
         new_leaves[0, :, columns] = (leaf_v[:, columns].astype(jnp.float32) - correct).astype(jnp.bfloat16)
 
     for dr in range(1, n_row):
-        x_copy(lax.rem(row + dr, n_row), row).wait_send()
         for j in range(chunks):
+            x_copy(j, lax.rem(row + dr, n_row), row).wait_send()
             fold_copy(j, lax.rem(row + dr, n_row), row).wait_send()
     for j in range(chunks):
         for h in range(halves):
@@ -218,9 +218,15 @@
             pass_copy(j, to_layer, to_col).wait_send()
 
 
-def finish(leaves, anc, leaves_out, anc_out):
-    leaves_out[...] = leaves[...]
-    anc_out[...] = anc[...]
+def finish(leaves, anc, leaves_out, anc_out, sem):
+    copies = [
+        pltpu.make_async_copy(anc, anc_out, sem.at[0]),
+        pltpu.make_async_copy(leaves, leaves_out, sem.at[1]),
+    ]
+    for copy in copies:
+        copy.start()
+    for copy in copies:
+        copy.wait()
 
 
 def shards(n_layer, n_row, n_col, leaf_sol, lower_blocks, lower_mask, upper_blocks, upper_mask, anc_rhs, diag_inv):
@@ -243,7 +249,7 @@
     )
     results = pl.pallas_call(
         functools.partial(kernel, n_layer, n_row, n_col, chunks),
-        out_shape=out_shape,
+        out_shape=(pltpu.VMEM(leaf_sol.shape, bf16), pltpu.VMEM(anc_rhs.shape, bf16)),
         in_specs=[anywhere, anywhere, scalars, anywhere, scalars, anywhere, anywhere],
         out_specs=(vmem, vmem),
         scratch_shapes=[
@@ -252,8 +258,8 @@
             pltpu.VMEM(upper_blocks.shape, bf16),
             pltpu.VMEM(anc_rhs.shape, bf16),
             pltpu.VMEM(diag_inv.shape, bf16),
-            pltpu.VMEM((n_row, strip, width), bf16),
-            pltpu.VMEM((n_row * strip // block, width, block), bf16),
+            pltpu.VMEM((chunks, n_row, strip, span), bf16),
+            pltpu.VMEM((chunks, n_row * strip // block, span, block), bf16),
             pltpu.VMEM((width, block), f32),
             pltpu.VMEM((chunks, halves, span, block), bf16),
             pltpu.VMEM((chunks, halves, span, block), bf16),
@@ -264,7 +270,7 @@
             pltpu.VMEM((chunks, n_row, strip, span), bf16),
             pltpu.VMEM((chunks, n_row, strip, span), bf16),
             *dma(
-                5, n_row, n_row, chunks * halves, chunks * halves,
+                5, chunks * n_row, chunks * n_row, chunks * halves, chunks * halves,
                 *[chunks * devices] * 5, chunks * n_row, chunks * n_row,
             ),
         ],
@@ -272,7 +278,15 @@
             collective_id=0, has_side_effects=True,
         ),
     )(leaf_sol, lower_blocks, lower_mask.T, upper_blocks, upper_mask, anc_rhs, diag_inv)
-    return pl.pallas_call(finish, out_shape=out_shape, in_specs=[vmem] * 2, out_specs=(vmem, vmem))(*results)
+    anyplace = pl.BlockSpec(memory_space=pl.ANY)
+    return pl.pallas_call(
+        finish,
+        out_shape=out_shape,
+        in_specs=[anyplace] * 2,
+        out_specs=(anyplace, anyplace),
+        scratch_shapes=dma(2),
+        compiler_params=pltpu.CompilerParams(vmem_limit_bytes=1024 * 1024),
+    )(*results)
 
 
 def solution(mesh):

time: 31.8 us -> 29 us (0.912)
  Pallas kernels: 31 us -> 28.2 us
    pallas_call x1, Pallas kernels: 29.4 us -> 27.6 us  [shards(): pl.pallas_call(functools.partial(kernel, n_layer, n_row, n_col, chunks),...]
    pallas_call x1, Pallas kernels: 1.59 us -> 0.68 us  [shards(): pl.pallas_call(finish, out_shape=out_shape, in_specs=[anyplace] * 2, out_...]
where the time goes in v3:
time: 29 us; the launch traced here: 28.9 us
  Pallas kernels  28.2 us (97%)
  between operations  0.64 us (2%)
    pallas_call x1, Pallas kernels, shards(): pl.pallas_call(functools.partial(kernel, n_layer, n_row, n_col, chunks),...  27.6 us
    pallas_call x1, Pallas kernels, shards(): pl.pallas_call(finish, out_shape=out_shape, in_specs=[anyplace] * 2, out_...  0.68 us

profile of v3, /device:TPU:0, one launch (start us, length us, event | category | flops | bytes accessed | tf_op | source)
XLA Modules:
  0.0 28.9 jit_solution(13027848558642658248)
XLA Ops:
  0.6 27.6 %shard_map.86 = (bf16[1,64,256]{2,1,0:T(8,128)(2,1)S(1)}, bf16[256,256]{1,0:T(8,128)(2,1)S(1)}) custom-call(bf16[1,64,256]{2,1,0:T(8,128)(2,1)} %leaf.1, bf16[1024,256]{1,0:T(8,128)(2,1)} %lower.1, s32[1,4]{1,0:T(1,128)} %bitcast.1, bf16[256,1024]{1,0:T(8,128)(2,1)} %upper.1, s32[1,4]{1,0:T(1,128)} %upper_mask.1, bf16[256,256]{1,0:T(8,128)(2,1)} %rhs.1, ...), custom_call_target="tpu_custom_call" | custom-call | tf_op jit(solution)/shard_map/pallas_call | solution.py:250
  28.2 0.7 %shard_map.87 = (bf16[1,64,256]{2,1,0:T(8,128)(2,1)}, bf16[256,256]{1,0:T(8,128)(2,1)}) custom-call(bf16[1,64,256]{2,1,0:T(8,128)(2,1)S(1)} %get-tuple-element.4.leaves, bf16[256,256]{1,0:T(8,128)(2,1)S(1)} %get-tuple-element.5.anc), custom_call_target="tpu_custom_call" | custom-call | tf_op jit(solution)/shard_map/pallas_call | solution.py:282

commit v4 on v3

--- a/solution.py
+++ b/solution.py
@@ -15,7 +15,7 @@
 
 
 def kernel(
-    n_layer, n_row, n_col, chunks,
+    n_layer, n_row, n_col, chunks, subs,
     leaf, lower, lower_mask, upper, upper_mask, rhs, inv,
     new_leaves, anc_out,
     leaf_v, lower_v, upper_v, rhs_v, inv_v, x_all, x_t, rhs_t,
@@ -34,6 +34,7 @@
     width = rhs_v.shape[1]
     span = width // chunks
     share = span // n_layer
+    piece = share // subs
     strip = leaf_v.shape[0]
     depth = n_row * strip
     devices = n_layer * n_col
@@ -95,15 +96,16 @@
             device_id=(layer, row, partner), device_id_type=MESH,
         )
 
-    def inside(index):
-        return pl.ds(pl.multiple_of(index * share, share), share)
-
-    def part_copy(j, to_layer, to_col, from_layer, from_col):
-        return pltpu.make_async_remote_copy(
-            src_ref=part.at[j, to_col // 2, inside(to_layer)],
-            dst_ref=part_in.at[j, from_layer * n_col + from_col],
-            send_sem=part_send.at[j * devices + to_layer * n_col + to_col],
-            recv_sem=part_recv.at[j * devices + from_layer * n_col + from_col],
+    def portion(index, s):
+        return pl.ds(pl.multiple_of(index * share + s * piece, piece), piece)
+
+    def part_copy(j, s, to_layer, to_col, from_layer, from_col):
+        base = (j * subs + s) * devices
+        return pltpu.make_async_remote_copy(
+            src_ref=part.at[j, to_col // 2, portion(to_layer, s)],
+            dst_ref=part_in.at[j, s, from_layer * n_col + from_col],
+            send_sem=part_send.at[base + to_layer * n_col + to_col],
+            recv_sem=part_recv.at[base + from_layer * n_col + from_col],
             device_id=(to_layer, row, to_col), device_id_type=MESH,
         )
 
@@ -122,46 +124,53 @@
             total = held[j, h] + pair_in[j, h].astype(jnp.float32)
             held[j, h] = total
             part[j, h] = total.astype(jnp.bfloat16)
-        for dl, dh in reversed(group):
-            part_copy(j, *peer(dl, dh), layer, col).start()
-
-    def anc_place(j, from_layer, from_col):
-        return anc_t.at[j, from_col, inside(from_layer)]
-
-    def anc_copy(j, to_layer, to_col, from_layer, from_col):
-        place = anc_place(j, from_layer, from_col)
+        for s in range(subs):
+            for dl, dh in reversed(group):
+                part_copy(j, s, *peer(dl, dh), layer, col).start()
+
+    def anc_place(j, s, from_layer, from_col):
+        return anc_t.at[j, from_col, portion(from_layer, s)]
+
+    def anc_copy(j, s, to_layer, to_col, from_layer, from_col):
+        place = anc_place(j, s, from_layer, from_col)
+        base = (j * subs + s) * devices
         return pltpu.make_async_remote_copy(
             src_ref=place, dst_ref=place,
-            send_sem=anc_send.at[j * devices + to_layer * n_col + to_col],
-            recv_sem=anc_recv.at[j * devices + from_layer * n_col + from_col],
+            send_sem=anc_send.at[base + to_layer * n_col + to_col],
+            recv_sem=anc_recv.at[base + from_layer * n_col + from_col],
             device_id=(to_layer, row, to_col), device_id_type=MESH,
         )
 
-    def pass_copy(j, from_layer, from_col):
-        place = anc_place(j, from_layer, from_col)
+    def pass_copy(j, s, from_layer, from_col):
+        place = anc_place(j, s, from_layer, from_col)
+        base = (j * subs + s) * devices
         return pltpu.make_async_remote_copy(
             src_ref=place, dst_ref=place,
-            send_sem=pass_send.at[j * devices + from_layer * n_col + from_col],
-            recv_sem=anc_recv.at[j * devices + from_layer * n_col + from_col],
+            send_sem=pass_send.at[base + from_layer * n_col + from_col],
+            recv_sem=anc_recv.at[base + from_layer * n_col + from_col],
             device_id=(layer, row, partner), device_id_type=MESH,
         )
 
     inverse = inv_v[...]
     for j in range(chunks):
-        remain = rhs_t[pl.ds(pl.multiple_of(j * span + layer * share, share), share), :] - held[j, half, inside(layer)]
-        for dl, dh in group:
-            from_layer, from_col = peer(dl, dh)
-            part_copy(j, layer, col, from_layer, from_col).wait_recv()
-            remain = remain - part_in[j, from_layer * n_col + from_col].astype(jnp.float32)
-        high = remain.astype(jnp.bfloat16)
-        rest = remain - high.astype(jnp.float32)
-        middle = rest.astype(jnp.bfloat16)
-        low = (rest - middle.astype(jnp.float32)).astype(jnp.bfloat16)
-        solved = dot_last(high, inverse) + (dot_last(middle, inverse) + dot_last(low, inverse))
-        anc_t[j, col, inside(layer)] = solved.astype(jnp.bfloat16)
-        for dl, dh in reversed(group):
-            anc_copy(j, *peer(dl, dh), layer, col).start()
-        pass_copy(j, layer, col).start()
+        for s in range(subs):
+            own = portion(layer, s)
+            place = pl.ds(pl.multiple_of(j * span + layer * share + s * piece, piece), piece)
+            remain = rhs_t[place, :] - held[j, half, own]
+            for dl, dh in group:
+                from_layer, from_col = peer(dl, dh)
+                part_copy(j, s, layer, col, from_layer, from_col).wait_recv()
+                remain = remain - part_in[j, s, from_layer * n_col + from_col].astype(jnp.float32)
+            high = remain.astype(jnp.bfloat16)
+            rest = remain - high.astype(jnp.float32)
+            middle = rest.astype(jnp.bfloat16)
+            low = (rest - middle.astype(jnp.float32)).astype(jnp.bfloat16)
+            terms = dot_last(jnp.concatenate([high, middle, low], axis=0), inverse)
+            solved = terms[:piece] + (terms[piece:2 * piece] + terms[2 * piece:])
+            anc_t[j, col, own] = solved.astype(jnp.bfloat16)
+            for dl, dh in reversed(group):
+                anc_copy(j, s, *peer(dl, dh), layer, col).start()
+            pass_copy(j, s, layer, col).start()
 
     def fold_copy(j, to_row, from_row):
         return pltpu.make_async_remote_copy(
@@ -172,17 +181,19 @@
 
     blocks_down = upper_v.shape[0] // block
     for j in range(chunks):
-        for dl, dh in group:
-            from_layer, from_col = peer(dl, dh)
-            anc_copy(j, layer, col, from_layer, from_col).wait_recv()
-            pass_copy(j, from_layer, from_col).start()
+        for s in range(subs):
+            for dl, dh in group:
+                from_layer, from_col = peer(dl, dh)
+                anc_copy(j, s, layer, col, from_layer, from_col).wait_recv()
+                pass_copy(j, s, from_layer, from_col).start()
         totals = [None] * blocks_down
         for parity in (side, other):
             for dh in range(halves):
                 from_col = lax.rem(half + dh, halves) * 2 + parity
                 if parity is other:
-                    for from_layer in range(n_layer):
-                        pass_copy(j, from_layer, from_col).wait_recv()
+                    for s in range(subs):
+                        for from_layer in range(n_layer):
+                            pass_copy(j, s, from_layer, from_col).wait_recv()
                 for i in range(blocks_down):
                     tile = upper_v[i * block:(i + 1) * block, pl.ds(pl.multiple_of(from_col * block, block), block)]
                     term = dot_last(tile, anc_t[j, from_col]) * upper_mask[i, from_col].astype(jnp.float32)
@@ -210,12 +221,13 @@
     for j in range(chunks):
         for h in range(halves):
             pair_copy(j, h).wait_send()
-        pass_copy(j, layer, col).wait_send()
-        for dl, dh in group:
-            to_layer, to_col = peer(dl, dh)
-            part_copy(j, to_layer, to_col, layer, col).wait_send()
-            anc_copy(j, to_layer, to_col, layer, col).wait_send()
-            pass_copy(j, to_layer, to_col).wait_send()
+        for s in range(subs):
+            pass_copy(j, s, layer, col).wait_send()
+            for dl, dh in group:
+                to_layer, to_col = peer(dl, dh)
+                part_copy(j, s, to_layer, to_col, layer, col).wait_send()
+                anc_copy(j, s, to_layer, to_col, layer, col).wait_send()
+                pass_copy(j, s, to_layer, to_col).wait_send()
 
 
 def finish(leaves, anc, leaves_out, anc_out, sem):
@@ -236,6 +248,7 @@
     chunks = 2
     span = width // chunks
     share = span // n_layer
+    subs = 2 if share >= 32 else 1
     halves = n_col // 2
     bf16, f32 = jnp.bfloat16, jnp.float32
     anywhere = pl.BlockSpec(memory_space=pltpu.HBM)
@@ -248,7 +261,7 @@
         jax.ShapeDtypeStruct(anc_rhs.shape, bf16),
     )
     results = pl.pallas_call(
-        functools.partial(kernel, n_layer, n_row, n_col, chunks),
+        functools.partial(kernel, n_layer, n_row, n_col, chunks, subs),
         out_shape=(pltpu.VMEM(leaf_sol.shape, bf16), pltpu.VMEM(anc_rhs.shape, bf16)),
         in_specs=[anywhere, anywhere, scalars, anywhere, scalars, anywhere, anywhere],
         out_specs=(vmem, vmem),
@@ -265,13 +278,13 @@
             pltpu.VMEM((chunks, halves, span, block), bf16),
             pltpu.VMEM((chunks, halves, span, block), f32),
             pltpu.VMEM((chunks, halves, span, block), bf16),
-            pltpu.VMEM((chunks, devices, share, block), bf16),
+            pltpu.VMEM((chunks, subs, devices, share // subs, block), bf16),
             pltpu.VMEM((chunks, n_col, span, block), bf16),
             pltpu.VMEM((chunks, n_row, strip, span), bf16),
             pltpu.VMEM((chunks, n_row, strip, span), bf16),
             *dma(
                 5, chunks * n_row, chunks * n_row, chunks * halves, chunks * halves,
-                *[chunks * devices] * 5, chunks * n_row, chunks * n_row,
+                *[chunks * subs * devices] * 5, chunks * n_row, chunks * n_row,
             ),
         ],
         compiler_params=pltpu.CompilerParams(

time: 29 us -> 29 us (level)
  no operation moved by 1% of the time
where the time goes in v4:
time: 29 us; the launch traced here: 28.8 us
  Pallas kernels  28.2 us (97%)
  between operations  0.64 us (2%)
    pallas_call x1, Pallas kernels, shards(): pl.pallas_call(functools.partial(kernel, n_layer, n_row, n_col, chunks, s...  27.5 us
    pallas_call x1, Pallas kernels, shards(): pl.pallas_call(finish, out_shape=out_shape, in_specs=[anyplace] * 2, out_...  0.68 us

profile of v4, /device:TPU:0, one launch (start us, length us, event | category | flops | bytes accessed | tf_op | source)
XLA Modules:
  0.0 28.8 jit_solution(12196604858641098135)
XLA Ops:
  0.6 27.5 %shard_map.86 = (bf16[1,64,256]{2,1,0:T(8,128)(2,1)S(1)}, bf16[256,256]{1,0:T(8,128)(2,1)S(1)}) custom-call(bf16[1,64,256]{2,1,0:T(8,128)(2,1)} %leaf.1, bf16[1024,256]{1,0:T(8,128)(2,1)} %lower.1, s32[1,4]{1,0:T(1,128)} %bitcast.1, bf16[256,1024]{1,0:T(8,128)(2,1)} %upper.1, s32[1,4]{1,0:T(1,128)} %upper_mask.1, bf16[256,256]{1,0:T(8,128)(2,1)} %rhs.1, ...), custom_call_target="tpu_custom_call" | custom-call | tf_op jit(solution)/shard_map/pallas_call | solution.py:263
  28.1 0.7 %shard_map.87 = (bf16[1,64,256]{2,1,0:T(8,128)(2,1)}, bf16[256,256]{1,0:T(8,128)(2,1)}) custom-call(bf16[1,64,256]{2,1,0:T(8,128)(2,1)S(1)} %get-tuple-element.4.leaves, bf16[256,256]{1,0:T(8,128)(2,1)S(1)} %get-tuple-element.5.anc), custom_call_target="tpu_custom_call" | custom-call | tf_op jit(solution)/shard_map/pallas_call | solution.py:295

commit v5 on v3

--- a/solution.py
+++ b/solution.py
@@ -16,9 +16,9 @@
 
 def kernel(
     n_layer, n_row, n_col, chunks,
-    leaf, lower, lower_mask, upper, upper_mask, rhs, inv,
+    leaf, lower, lower_marks, upper, upper_marks, rhs, inv,
     new_leaves, anc_out,
-    leaf_v, lower_v, upper_v, rhs_v, inv_v, x_all, x_t, rhs_t,
+    lower_mask, upper_mask, leaf_v, lower_v, upper_v, rhs_v, inv_v, x_all, x_t, rhs_t,
     pair_out, pair_in, held, part, part_in, anc_t, fold, fold_in,
     local_sem, x_send, x_recv, pair_send, pair_recv, part_send, part_recv,
     anc_send, pass_send, anc_recv, fold_send, fold_recv,
@@ -42,15 +42,6 @@
     def peer(dl, dh):
         return lax.rem(layer + dl, n_layer), lax.rem(half + dh, halves) * 2 + side
 
-    loads = [
-        pltpu.make_async_copy(source, target, local_sem.at[index])
-        for index, (source, target) in enumerate(
-            ((leaf.at[0], leaf_v), (lower, lower_v), (rhs, rhs_v), (inv, inv_v), (upper, upper_v))
-        )
-    ]
-    for load in loads:
-        load.start()
-
     barrier = pltpu.get_barrier_semaphore()
     for dr in reversed(range(1, n_row)):
         pl.semaphore_signal(barrier, inc=1, device_id=(layer, lax.rem(row + dr, n_row), col), device_id_type=MESH)
@@ -58,11 +49,23 @@
         to_layer, to_col = peer(dl, dh)
         pl.semaphore_signal(barrier, inc=1, device_id=(to_layer, row, to_col), device_id_type=MESH)
     pl.semaphore_signal(barrier, inc=1, device_id=(layer, row, partner), device_id_type=MESH)
+    loads = [
+        pltpu.make_async_copy(source, target, local_sem.at[index])
+        for index, (source, target) in enumerate(
+            (
+                (leaf.at[0], leaf_v), (lower, lower_v), (rhs, rhs_v), (inv, inv_v), (upper, upper_v),
+                (lower_marks, lower_mask), (upper_marks, upper_mask),
+            )
+        )
+    ]
+    for load in loads:
+        load.start()
+    loads[0].wait()
     pl.semaphore_wait(barrier, n_row + len(group))
 
     def x_copy(j, to_row, from_row):
         return pltpu.make_async_remote_copy(
-            src_ref=leaf.at[0, :, pl.ds(j * span, span)], dst_ref=x_all.at[j, from_row],
+            src_ref=leaf_v.at[:, pl.ds(j * span, span)], dst_ref=x_all.at[j, from_row],
             send_sem=x_send.at[j * n_row + to_row], recv_sem=x_recv.at[j * n_row + from_row],
             device_id=(layer, to_row, col), device_id_type=MESH,
         )
@@ -70,14 +73,14 @@
     for j in range(chunks):
         for dr in range(1, n_row):
             x_copy(j, lax.rem(row + dr, n_row), row).start()
-    loads[0].wait()
     for j in range(chunks):
         x_all[j, row] = leaf_v[:, j * span:(j + 1) * span]
     loads[2].wait()
     rhs_t[...] = rhs_v[...].astype(jnp.float32).T
     loads[1].wait()
     loads[3].wait()
-    loads[4].wait()
+    for load in loads[4:]:
+        load.wait()
     strips = block // strip
 
     def partial_sum(j, to_col):
@@ -239,7 +242,7 @@
     halves = n_col // 2
     bf16, f32 = jnp.bfloat16, jnp.float32
     anywhere = pl.BlockSpec(memory_space=pltpu.HBM)
-    scalars = pl.BlockSpec(memory_space=pltpu.SMEM)
+    lower_marks = lower_mask.T
     vmem = pl.BlockSpec(memory_space=pltpu.VMEM)
     devices = n_layer * n_col
     dma = lambda *sizes: [pltpu.SemaphoreType.DMA((size,)) for size in sizes]
@@ -250,9 +253,11 @@
     results = pl.pallas_call(
         functools.partial(kernel, n_layer, n_row, n_col, chunks),
         out_shape=(pltpu.VMEM(leaf_sol.shape, bf16), pltpu.VMEM(anc_rhs.shape, bf16)),
-        in_specs=[anywhere, anywhere, scalars, anywhere, scalars, anywhere, anywhere],
+        in_specs=[anywhere] * 7,
         out_specs=(vmem, vmem),
         scratch_shapes=[
+            pltpu.SMEM(lower_marks.shape, jnp.int32),
+            pltpu.SMEM(upper_mask.shape, jnp.int32),
             pltpu.VMEM((strip, width), bf16),
             pltpu.VMEM(lower_blocks.shape, bf16),
             pltpu.VMEM(upper_blocks.shape, bf16),
@@ -270,14 +275,14 @@
             pltpu.VMEM((chunks, n_row, strip, span), bf16),
             pltpu.VMEM((chunks, n_row, strip, span), bf16),
             *dma(
-                5, chunks * n_row, chunks * n_row, chunks * halves, chunks * halves,
+                7, chunks * n_row, chunks * n_row, chunks * halves, chunks * halves,
                 *[chunks * devices] * 5, chunks * n_row, chunks * n_row,
             ),
         ],
         compiler_params=pltpu.CompilerParams(
             collective_id=0, has_side_effects=True,
         ),
-    )(leaf_sol, lower_blocks, lower_mask.T, upper_blocks, upper_mask, anc_rhs, diag_inv)
+    )(leaf_sol, lower_blocks, lower_marks, upper_blocks, upper_mask, anc_rhs, diag_inv)
     anyplace = pl.BlockSpec(memory_space=pl.ANY)
     return pl.pallas_call(
         finish,

time: 29 us -> 28.2 us (0.972)
  Pallas kernels: 28.2 us -> 27.4 us
    pallas_call x1, Pallas kernels: 27.6 us -> 26.7 us  [shards(): pl.pallas_call(functools.partial(kernel, n_layer, n_row, n_col, chunks),...]
where the time goes in v5:
time: 28.2 us; the launch traced here: 28 us
  Pallas kernels  27.4 us (97%)
  between operations  0.64 us (2%)
    pallas_call x1, Pallas kernels, shards(): pl.pallas_call(functools.partial(kernel, n_layer, n_row, n_col, chunks),...  26.7 us
    pallas_call x1, Pallas kernels, shards(): pl.pallas_call(finish, out_shape=out_shape, in_specs=[anyplace] * 2, out_...  0.68 us

profile of v5, /device:TPU:0, one launch (start us, length us, event | category | flops | bytes accessed | tf_op | source)
XLA Modules:
  0.0 28.0 jit_solution(11760801231108718064)
XLA Ops:
  0.6 26.7 %shard_map.86 = (bf16[1,64,256]{2,1,0:T(8,128)(2,1)S(1)}, bf16[256,256]{1,0:T(8,128)(2,1)S(1)}) custom-call(bf16[1,64,256]{2,1,0:T(8,128)(2,1)} %leaf.1, bf16[1024,256]{1,0:T(8,128)(2,1)} %lower.1, s32[1,4]{1,0:T(1,128)} %bitcast.1, bf16[256,1024]{1,0:T(8,128)(2,1)} %upper.1, s32[1,4]{1,0:T(1,128)} %upper_marks.1, bf16[256,256]{1,0:T(8,128)(2,1)} %rhs.1, ...), custom_call_target="tpu_custom_call" | custom-call | tf_op jit(solution)/shard_map/pallas_call | solution.py:253
  27.4 0.7 %shard_map.87 = (bf16[1,64,256]{2,1,0:T(8,128)(2,1)}, bf16[256,256]{1,0:T(8,128)(2,1)}) custom-call(bf16[1,64,256]{2,1,0:T(8,128)(2,1)S(1)} %get-tuple-element.4.leaves, bf16[256,256]{1,0:T(8,128)(2,1)S(1)} %get-tuple-element.5.anc), custom_call_target="tpu_custom_call" | custom-call | tf_op jit(solution)/shard_map/pallas_call | solution.py:287

commit v6 on v5

--- a/solution.py
+++ b/solution.py
@@ -115,18 +115,20 @@
             x_copy(j, row, lax.rem(row + dr, n_row)).wait_recv()
         for k in range(depth // block):
             x_t[j, k] = x_all[j, k * strips:(k + 1) * strips].reshape(block, span).T
-        for h in range(halves):
+        turns = [(dh, lax.rem(half + dh, halves)) for dh in reversed(range(halves))]
+        for _, h in turns:
             pair_out[j, h] = partial_sum(j, h * 2 + other).astype(jnp.bfloat16)
             pair_copy(j, h).start()
-        for h in range(halves):
+        for _, h in turns:
             held[j, h] = partial_sum(j, h * 2 + side)
-        for h in range(halves):
+        for turn, h in turns:
             pair_copy(j, h).wait_recv()
             total = held[j, h] + pair_in[j, h].astype(jnp.float32)
             held[j, h] = total
             part[j, h] = total.astype(jnp.bfloat16)
-        for dl, dh in reversed(group):
-            part_copy(j, *peer(dl, dh), layer, col).start()
+            for dl, dh in reversed(group):
+                if dh == turn:
+                    part_copy(j, *peer(dl, dh), layer, col).start()
 
     def anc_place(j, from_layer, from_col):
         return anc_t.at[j, from_col, inside(from_layer)]
@@ -160,7 +162,8 @@
         rest = remain - high.astype(jnp.float32)
         middle = rest.astype(jnp.bfloat16)
         low = (rest - middle.astype(jnp.float32)).astype(jnp.bfloat16)
-        solved = dot_last(high, inverse) + (dot_last(middle, inverse) + dot_last(low, inverse))
+        terms = dot_last(jnp.concatenate([high, middle, low], axis=0), inverse)
+        solved = terms[:share] + (terms[share:2 * share] + terms[2 * share:])
         anc_t[j, col, inside(layer)] = solved.astype(jnp.bfloat16)
         for dl, dh in reversed(group):
             anc_copy(j, *peer(dl, dh), layer, col).start()

time: 28.2 us -> 28.1 us (level)
  no operation moved by 1% of the time
where the time goes in v6:
time: 28.1 us; the launch traced here: 27.9 us
  Pallas kernels  27.3 us (97%)
  between operations  0.64 us (2%)
    pallas_call x1, Pallas kernels, shards(): pl.pallas_call(functools.partial(kernel, n_layer, n_row, n_col, chunks),...  26.6 us
    pallas_call x1, Pallas kernels, shards(): pl.pallas_call(finish, out_shape=out_shape, in_specs=[anyplace] * 2, out_...  0.68 us

profile of v6, /device:TPU:0, one launch (start us, length us, event | category | flops | bytes accessed | tf_op | source)
XLA Modules:
  0.0 27.9 jit_solution(2638924167930905855)
XLA Ops:
  0.6 26.6 %shard_map.86 = (bf16[1,64,256]{2,1,0:T(8,128)(2,1)S(1)}, bf16[256,256]{1,0:T(8,128)(2,1)S(1)}) custom-call(bf16[1,64,256]{2,1,0:T(8,128)(2,1)} %leaf.1, bf16[1024,256]{1,0:T(8,128)(2,1)} %lower.1, s32[1,4]{1,0:T(1,128)} %bitcast.1, bf16[256,1024]{1,0:T(8,128)(2,1)} %upper.1, s32[1,4]{1,0:T(1,128)} %upper_marks.1, bf16[256,256]{1,0:T(8,128)(2,1)} %rhs.1, ...), custom_call_target="tpu_custom_call" | custom-call | tf_op jit(solution)/shard_map/pallas_call | solution.py:256
  27.2 0.7 %shard_map.87 = (bf16[1,64,256]{2,1,0:T(8,128)(2,1)}, bf16[256,256]{1,0:T(8,128)(2,1)}) custom-call(bf16[1,64,256]{2,1,0:T(8,128)(2,1)S(1)} %get-tuple-element.4.leaves, bf16[256,256]{1,0:T(8,128)(2,1)S(1)} %get-tuple-element.5.anc), custom_call_target="tpu_custom_call" | custom-call | tf_op jit(solution)/shard_map/pallas_call | solution.py:290
